TPU v7x, 256 devices: a whole 4x4x8 slice. The times are simulated.
256 devices in a mesh: row: 16 (over z, core), col: 8 (over x_hi, y), feat: 2 (over x_lo).
Axes of the slice: x: 4 (x_hi: 2, x_lo: 2; x = x_hi * 2 + x_lo), y: 4, z: 8, core: 2. Of those that a mesh axis runs over, the one named last changes fastest.
Arguments:
- features: bfloat16 [65536, 256], P(('col', 'row'), 'feat'), may hold values from -6 to 6
- tile_rows: int32 [16, 8, 256], P('row', 'col'), may hold values from 0 to 31, as said below
- tile_cols: int32 [16, 8, 256], P('row', 'col'), may hold values from 0 to 63
- tile_count: int32 [16, 8], P('row', 'col'), may hold values from 64 to 256, as said below
- tile_values: bfloat16 [16, 8, 256, 128, 128], P('row', 'col'), may hold values from -0.21875 to 0.21875
- weights: bfloat16 [256, 256], replicated, may hold values from -0.375 to 0.375
- cotangent: bfloat16 [65536, 256], P(('row', 'col'), 'feat'), may hold values from -6 to 6
Outputs:
- activated: bfloat16 [65536, 256], P(('row', 'col'), 'feat')
- feature_grad: bfloat16 [65536, 256], P(('col', 'row'), 'feat')
- weight_grad: float32 [256, 256], P('feat')
Inputs may be any that keep to these rules, and one draw needn't show every extreme that they name: `tile_rows`: block rows of a cell, unevenly loaded. `tile_count`: some cell has all 256 slots live.
All inputs are finite; a program needn't handle non-finite values.
Results may differ from a plain program's by a relative error of at most 0.027.
Values may be sent and summed in bfloat16 or wider, within the bound.
A program may use at most 128 MiB of HBM per device.

v0:
```python
import jax
import jax.numpy as jnp
from jax import lax
from jax.sharding import PartitionSpec as P


def shards(features, tile_rows, tile_cols, tile_count, tile_values, weights, cotangent):
    width = tile_values.shape[-1]
    slots = tile_values.shape[2]
    local_tiles = tile_values[0, 0]
    block_rows = tile_rows[0, 0]
    block_cols = tile_cols[0, 0]
    live_mask = (jnp.arange(slots) < tile_count[0, 0]).astype(jnp.float32)
    n_rowdev = lax.axis_size("row")
    n_coldev = lax.axis_size("col")
    local_blocks = features.shape[0] // width
    feat_half = features.shape[1]
    feat_index = lax.axis_index("feat")
    row_blocks = local_blocks * n_coldev
    col_blocks = local_blocks * n_rowdev
    node_total = features.shape[0] * n_rowdev * n_coldev
    panel = lax.all_gather(features, "row", axis=0, tiled=True)
    gathered = panel.reshape(col_blocks, width, feat_half)[block_cols]
    products = jnp.einsum("tij,tjf->tif", local_tiles, gathered, preferred_element_type=jnp.float32)
    products = products * live_mask[:, None, None]
    partial_value = (
        jnp.zeros((row_blocks, width, feat_half), jnp.float32).at[block_rows].add(products)
    )
    summed = lax.psum_scatter(
        partial_value.reshape(row_blocks * width, feat_half).astype(jnp.bfloat16),
        "col",
        scatter_dimension=0,
        tiled=True,
    )
    weight_rows = lax.dynamic_slice_in_dim(weights, feat_index * feat_half, feat_half, 0)
    mix_term = jnp.dot(summed, weight_rows, preferred_element_type=jnp.float32)
    hidden = lax.psum_scatter(
        mix_term.astype(jnp.bfloat16), "feat", scatter_dimension=1, tiled=True
    ).astype(jnp.float32)
    negative = jnp.minimum(hidden, 0.0)
    activated = jnp.where(hidden > 0, hidden, jnp.expm1(negative)).astype(jnp.bfloat16)
    slope_factor = jnp.where(hidden > 0, 1.0, jnp.exp(negative))
    grad_out = (cotangent.astype(jnp.float32) * slope_factor).astype(jnp.bfloat16)
    grad_whole = lax.all_gather(grad_out, "feat", axis=1, tiled=True)
    weight_term = lax.dot_general(
        summed, grad_whole, (((0,), (0,)), ((), ())), preferred_element_type=jnp.float32
    )
    n_feat = lax.axis_size("feat")
    slots = jnp.zeros((n_feat,) + weight_term.shape, jnp.float32)
    slots = lax.dynamic_update_slice_in_dim(slots, weight_term[None], feat_index, 0)
    slots = lax.psum(slots, ("row", "col", "feat"))
    weight_grad = lax.dynamic_index_in_dim(slots, feat_index, 0, keepdims=False) * node_total ** (
        -0.5
    )
    spread = lax.dot_general(
        grad_whole, weight_rows, (((1,), (1,)), ((), ())), preferred_element_type=jnp.float32
    ).astype(jnp.bfloat16)
    spread_panel = lax.all_gather(spread, "col", axis=0, tiled=True)
    spread_blocks = spread_panel.reshape(row_blocks, width, feat_half)[block_rows]
    back_products = jnp.einsum(
        "tji,tjf->tif", local_tiles, spread_blocks, preferred_element_type=jnp.float32
    )
    back_products = back_products * live_mask[:, None, None]
    back_partial = (
        jnp.zeros((col_blocks, width, feat_half), jnp.float32).at[block_cols].add(back_products)
    )
    back_summed = lax.psum_scatter(
        back_partial.reshape(col_blocks * width, feat_half).astype(jnp.bfloat16),
        "row",
        scatter_dimension=0,
        tiled=True,
    )
    return (activated, back_summed, weight_grad)


def solution(mesh):
    return jax.shard_map(
        shards,
        mesh=mesh,
        in_specs=(
            P(("col", "row"), "feat"),
            P("row", "col", None),
            P("row", "col", None),
            P("row", "col"),
            P("row", "col", None, None, None),
            P(),
            P(("row", "col"), "feat"),
        ),
        out_specs=(P(("row", "col"), "feat"), P(("col", "row"), "feat"), P("feat", None)),
        check_vma=False,
    )
```

profile of v0, /device:TPU:2, one launch (start us, length us, event | category | flops | bytes accessed | tf_op | source)
XLA Modules:
  0.0 605.1 jit_solution(15216501221385841070)
XLA Ops:
  7.2 0.0 copy-start
  7.2 0.0 all-gather.3.cloned.1.call-start
  7.2 0.7 all-gather.3.cloned.1.call-update
  7.9 0.0 reduce-scatter.6.cloned.1.call-start
  8.6 0.7 compare_select_fusion
  9.3 43.2 %all-gather.3.cloned.1.call-done = bf16[8192,128]{1,0:T(8,128)(2,1)} async-done(((bf16[512,128]{1,0:T(8,128)(2,1)}), bf16[8192,128]{1,0:T(8,128)(2,1)}) %all-gather.3.cloned.1.call-update) | async-done | bytes 2097168 | tf_op jit(solution)/shard_map/all_gather | solution.py:22
  52.6 10.2 %gather_fusion = bf16[256,128,128]{2,1,0:T(8,128)(2,1)} fusion(bf16[64,128,128]{2,1,0:T(8,128)(2,1)} %bitcast.36, s32[1024]{0:T(1024)S(1)} %pad_clamp_fusion.1), kind=kCustom, calls=%fused_computation | custom fusion | bytes 16778240 | tf_op jit(solution)/shard_map/gather | solution.py:23
  62.8 13.0 %multiply_bitcast_fusion.1 = f32[256,128,128]{1,2,0:T(8,128)} fusion(bf16[256,128,128]{2,1,0:T(8,128)(2,1)} %gather_fusion, bf16[1,1,256,128,128]{4,3,2,1,0:T(8,128)(2,1)} %param.11, f32[256]{0:T(256)S(1)} %compare_convert_fusion), kind=kOutput, calls=%fused_computation.5 | convolution fusion | flops 1077936128 | bytes 33555456 | tf_op jit(solution)/shard_map/tij,tjf->tif/dot_general | solution.py:24
  75.8 17.4 %copy.17 = f32[256,128,128]{2,1,0:T(8,128)} copy(f32[256,128,128]{1,2,0:T(8,128)} %multiply_bitcast_fusion.1) | data formatting | bytes 33554432 | tf_op jit(solution)/shard_map/mul | solution.py:25
  93.2 0.2 broadcast_in_dim.22
  93.5 0.0 copy-start.3
  93.5 33.2 %scatter_fusion = f32[32,128,128]{2,1,0:T(8,128)S(1)} fusion(f32[32,128,128]{2,1,0:T(8,128)S(1)} %broadcast_in_dim.22, s32[256]{0:T(256)S(1)} %bitcast.43, f32[256,128,128]{2,1,0:T(8,128)} %copy.17), kind=kCustom, calls=%fused_computation.2 | custom fusion | flops 4194304 | bytes 50332672 | tf_op jit(solution)/shard_map/scatter-add | solution.py:27
  126.7 1.1 convert_element_type.38
  127.8 0.0 reduce-scatter.6.cloned.1.call-update
  127.8 0.0 reduce-scatter.10.cloned.1.call-start
  127.9 74.5 %reduce-scatter.6.cloned.1.call-done = bf16[512,128]{1,0:T(8,128)(2,1)} async-done(((bf16[4096,128]{1,0:T(8,128)(2,1)}), bf16[512,128]{1,0:T(8,128)(2,1)}) %reduce-scatter.6.cloned.1.call-update) | async-done | bytes 131088 | tf_op jit(solution)/shard_map/reduce_scatter | solution.py:29
  202.3 0.0 copy-done
  202.4 1.1 convolution_convert_fusion
  203.5 0.8 copy.22
  204.3 0.0 reduce-scatter.10.cloned.1.call-update
  204.3 0.0 all-gather.5.cloned.1.call-start
  204.4 16.0 %reduce-scatter.10.cloned.1.call-done = bf16[128,512]{1,0:T(8,128)(2,1)} async-done(((bf16[256,512]{1,0:T(8,128)(2,1)}), bf16[128,512]{1,0:T(8,128)(2,1)}) %reduce-scatter.10.cloned.1.call-update) | async-done | bytes 131088
  220.4 1.0 copy.23
  221.4 0.0 copy-done.3
  221.5 0.8 fusion.7
  222.3 5.9 all_gather.10
  228.2 0.9 convolution_convert_fusion.1
  229.0 0.0 all-gather.5.cloned.1.call-update
  229.1 0.0 all-reduce.2.cloned.1.call-start
  229.2 1.1 fusion.2
  230.3 0.0 copy-start.2
  230.3 0.7 copy-done.2
  231.0 0.0 all-reduce.2.cloned.1.call-update
  231.0 0.2 reduce-scatter.8.cloned.1.call-start
  231.3 50.6 %all-gather.5.cloned.1.call-done = bf16[4096,128]{1,0:T(8,128)(2,1)} async-done(((bf16[512,128]{1,0:T(8,128)(2,1)}), bf16[4096,128]{1,0:T(8,128)(2,1)}) %all-gather.5.cloned.1.call-update) | async-done | bytes 1048592 | tf_op jit(solution)/shard_map/all_gather | solution.py:58
  281.9 9.8 %gather_fusion.1 = bf16[256,128,128]{2,1,0:T(8,128)(2,1)} fusion(bf16[32,128,128]{2,1,0:T(8,128)(2,1)} %bitcast.35, s32[1024]{0:T(1024)S(1)} %pad_clamp_fusion), kind=kCustom, calls=%fused_computation.1 | custom fusion | bytes 16778240 | tf_op jit(solution)/shard_map/gather | solution.py:59
  291.7 15.4 %multiply_bitcast_fusion = f32[256,128,128]{1,2,0:T(8,128)} fusion(bf16[256,128,128]{2,1,0:T(8,128)(2,1)} %gather_fusion.1, bf16[1,1,256,128,128]{4,3,2,1,0:T(8,128)(2,1)} %param.11, f32[256]{0:T(256)S(1)} %compare_convert_fusion), kind=kOutput, calls=%fused_computation.4 | convolution fusion | flops 1077936128 | bytes 33555456 | tf_op jit(solution)/shard_map/tji,tjf->tif/dot_general | solution.py:60
  307.1 17.5 %copy.19 = f32[256,128,128]{2,1,0:T(8,128)} copy(f32[256,128,128]{1,2,0:T(8,128)} %multiply_bitcast_fusion) | data formatting | bytes 33554432 | tf_op jit(solution)/shard_map/mul | solution.py:63
  324.6 2.5 broadcast_in_dim.23
  327.0 0.0 copy-start.1
  327.0 52.1 %scatter_fusion.1 = f32[64,128,128]{2,1,0:T(8,128)} fusion(f32[64,128,128]{2,1,0:T(8,128)} %broadcast_in_dim.23, s32[256]{0:T(256)S(1)} %bitcast.42, f32[256,128,128]{2,1,0:T(8,128)} %copy.19), kind=kCustom, calls=%fused_computation.3 | custom fusion | flops 4194304 | bytes 50332672 | tf_op jit(solution)/shard_map/scatter-add | solution.py:65
  379.1 3.9 convert_element_type.46
  383.0 0.0 reduce-scatter.8.cloned.1.call-update
  383.1 154.2 %all-reduce.2.cloned.1.call-done = f32[2,128,256]{2,1,0:T(8,128)} async-done(((f32[2,128,256]{2,1,0:T(8,128)}), f32[2,128,256]{2,1,0:T(8,128)}) %all-reduce.2.cloned.1.call-update) | async-done | bytes 262160 | tf_op jit(solution)/shard_map/psum | solution.py:51
  537.3 1.6 multiply_bitcast_fusion.2
  538.8 59.4 %reduce-scatter.8.cloned.1.call-done = bf16[512,128]{1,0:T(8,128)(2,1)} async-done(((bf16[8192,128]{1,0:T(8,128)(2,1)}), bf16[512,128]{1,0:T(8,128)(2,1)}) %reduce-scatter.8.cloned.1.call-update) | async-done | bytes 131088 | tf_op jit(solution)/shard_map/reduce_scatter | solution.py:67
  598.3 0.0 copy-done.1
  (4 shorter events, 0.0 us)
Async XLA Ops:
  7.2 195.2 %copy-start = (bf16[256,256]{1,0:T(8,128)(2,1)S(1)}, bf16[256,256]{1,0:T(8,128)(2,1)}, u32[]{:S(2)}) copy-start(bf16[256,256]{1,0:T(8,128)(2,1)} %param.12) | copy-start | bytes 393220
  7.2 45.4 %all-gather.3.cloned.1.call-start = ((), (), s32[]{:S(2)}) async-start(), calls=%async_computation.3 | async-start | bytes 2228224 | tf_op jit(solution)/shard_map/all_gather | solution.py:22
  7.9 194.4 %reduce-scatter.6.cloned.1.call-start = ((), (), s32[]{:S(2)}) async-start(), calls=%async_computation.4 | async-start | bytes 1179648 | tf_op jit(solution)/shard_map/reduce_scatter | solution.py:29
  93.5 128.0 %copy-start.3 = (bf16[512,128]{1,0:T(8,128)(2,1)S(1)}, bf16[512,128]{1,0:T(8,128)(2,1)}, u32[]{:S(2)}) copy-start(bf16[512,128]{1,0:T(8,128)(2,1)} %param.13) | copy-start | bytes 393220
  127.8 92.6 %reduce-scatter.10.cloned.1.call-start = ((), (), s32[]{:S(2)}) async-start(), calls=%async_computation.8 | async-start | bytes 393216
  204.3 77.5 %all-gather.5.cloned.1.call-start = ((), (), s32[]{:S(2)}) async-start(), calls=%async_computation.5 | async-start | bytes 1179648 | tf_op jit(solution)/shard_map/all_gather | solution.py:58
  229.1 308.2 %all-reduce.2.cloned.1.call-start = ((), (), s32[]{:S(2)}) async-start(), calls=%async_computation.7 | async-start | bytes 524288 | tf_op jit(solution)/shard_map/psum | solution.py:51
  230.3 0.7 copy-start.2
  231.0 367.2 %reduce-scatter.8.cloned.1.call-start = ((), (), s32[]{:S(2)}) async-start(), calls=%async_computation.6 | async-start | bytes 2228224 | tf_op jit(solution)/shard_map/reduce_scatter | solution.py:67
  327.0 271.2 %copy-start.1 = (bf16[256,256]{1,0:T(8,128)(2,1)S(1)}, bf16[256,256]{1,0:T(8,128)(2,1)}, u32[]{:S(2)}) copy-start(bf16[256,256]{1,0:T(8,128)(2,1)} %param.12) | copy-start | bytes 393220
Sparse Core Ops, SparseCore 0:
  9.8 42.6 all-gather.2
  127.9 74.3 reduce-scatter.5
  205.0 15.3 reduce-scatter.9
  229.2 52.6 all-gather.4
  287.2 250.0 all-reduce.1
  540.2 57.9 reduce-scatter.7
where the time goes:
time: 607 us; the launch traced here: 605 us
  waiting for transfers between devices  399 us (66%)
  other arithmetic  93.4 us (15%)
  local copies, waits for them, and re-layouts  60.2 us (10%)
  matrix products  31.5 us (5%)
  between operations  14.9 us (2%)
    psum x1, waiting for transfers between devices, shards(): slots = lax.psum(slots, ('row', 'col', 'feat'))  154 us
    reduce_scatter x1, waiting for transfers between devices, shards(): lax.psum_scatter(partial_value.reshape(row_blocks * width, feat_half).ast...  74.5 us
    reduce_scatter x1, waiting for transfers between devices, shards(): lax.psum_scatter(back_partial.reshape(col_blocks * width, feat_half).asty...  59.4 us
    scatter-add x1, other arithmetic, shards(): jnp.zeros((col_blocks, width, feat_half), jnp.float32).at[block_cols]  52.1 us
    all_gather x1, waiting for transfers between devices, shards(): spread_panel = lax.all_gather(spread, 'col', axis=0, tiled=True)  50.6 us
    all_gather x1, waiting for transfers between devices, shards(): panel = lax.all_gather(features, 'row', axis=0, tiled=True)  43.2 us
    scatter-add x1, other arithmetic, shards(): jnp.zeros((row_blocks, width, feat_half), jnp.float32).at[block_rows]  33.2 us
    mul x1, local copies, waits for them, and re-layouts, shards(): back_products = back_products * live_mask[:, None, None]  17.5 us
  transfers between devices with their start and end apart: 6, of which 6 were waited for; matrix products, arithmetic and copies ran while one was open for 17% of the time, Pallas kernels for 0%

commit v1 on v0

--- a/solution.py
+++ b/solution.py
@@ -48,7 +48,7 @@
     n_feat = lax.axis_size("feat")
     slots = jnp.zeros((n_feat,) + weight_term.shape, jnp.float32)
     slots = lax.dynamic_update_slice_in_dim(slots, weight_term[None], feat_index, 0)
-    slots = lax.psum(slots, ("row", "col", "feat"))
+    slots = jnp.sum(lax.all_gather(slots, ("row", "col", "feat")), axis=0)
     weight_grad = lax.dynamic_index_in_dim(slots, feat_index, 0, keepdims=False) * node_total ** (
         -0.5
     )

time: 607 us -> 1150 us (1.89)
  waiting for transfers between devices: 399 us -> 923 us
  other arithmetic: 93.4 us -> 114 us
    all_gather x0 -> x1, waiting for transfers between devices: none -> 695 us  [shards(): slots = jnp.sum(lax.all_gather(slots, ('row', 'col', 'feat')), axis=0)]
    psum x1 -> x0, waiting for transfers between devices: 154 us -> none  [shards(): slots = lax.psum(slots, ('row', 'col', 'feat'))]
    reduce_sum x0 -> x1, other arithmetic: none -> 21.2 us  [shards(): slots = jnp.sum(lax.all_gather(slots, ('row', 'col', 'feat')), axis=0)]
    reduce_scatter x1, waiting for transfers between devices: 59.4 us -> 43.4 us  [shards(): lax.psum_scatter(back_partial.reshape(col_blocks * width, feat_half).asty...]
  transfers between devices with their start and end apart: 6 -> 6, of which waited for: 6 -> 6; matrix products, arithmetic and copies ran while one was open for 17% -> 11% of each run, Pallas kernels for 0% -> 0%
where the time goes in v1:
time: 1150 us
  waiting for transfers between devices  923 us (80%)
  other arithmetic  114 us (10%)
  local copies, waits for them, and re-layouts  60.3 us (5%)
  matrix products  31.7 us (3%)
  between operations  14.9 us (1%)
    all_gather x1, waiting for transfers between devices, shards(): slots = jnp.sum(lax.all_gather(slots, ('row', 'col', 'feat')), axis=0)  695 us
    reduce_scatter x1, waiting for transfers between devices, shards(): lax.psum_scatter(partial_value.reshape(row_blocks * width, feat_half).ast...  74.5 us
    scatter-add x1, other arithmetic, shards(): jnp.zeros((col_blocks, width, feat_half), jnp.float32).at[block_cols]  52.3 us
    all_gather x1, waiting for transfers between devices, shards(): spread_panel = lax.all_gather(spread, 'col', axis=0, tiled=True)  50.6 us
    reduce_scatter x1, waiting for transfers between devices, shards(): lax.psum_scatter(back_partial.reshape(col_blocks * width, feat_half).asty...  43.4 us
    all_gather x1, waiting for transfers between devices, shards(): panel = lax.all_gather(features, 'row', axis=0, tiled=True)  43.2 us
    scatter-add x1, other arithmetic, shards(): jnp.zeros((row_blocks, width, feat_half), jnp.float32).at[block_rows]  33.2 us
  transfers between devices with their start and end apart: 6, of which 6 were waited for; matrix products, arithmetic and copies ran while one was open for 11% of the time, Pallas kernels for 0%

profile of v1, /device:TPU:2, one launch (start us, length us, event | category | flops | bytes accessed | tf_op | source)
XLA Modules:
  0.0 1150.6 jit_solution(13731714298730656000)
XLA Ops:
  7.2 0.0 copy-start
  7.2 0.0 all-gather.4.cloned.1.call-start
  7.2 0.7 all-gather.4.cloned.1.call-update
  7.9 0.0 reduce-scatter.6.cloned.1.call-start
  8.6 0.7 compare_select_fusion
  9.3 43.2 %all-gather.4.cloned.1.call-done = bf16[8192,128]{1,0:T(8,128)(2,1)} async-done(((bf16[512,128]{1,0:T(8,128)(2,1)}), bf16[8192,128]{1,0:T(8,128)(2,1)}) %all-gather.4.cloned.1.call-update) | async-done | bytes 2097168 | tf_op jit(solution)/shard_map/all_gather | solution.py:22
  52.6 10.2 gather_fusion
  62.8 13.0 %multiply_bitcast_fusion.1 = f32[256,128,128]{1,2,0:T(8,128)} fusion(bf16[256,128,128]{2,1,0:T(8,128)(2,1)} %gather_fusion, bf16[1,1,256,128,128]{4,3,2,1,0:T(8,128)(2,1)} %param.11, f32[256]{0:T(256)S(1)} %compare_convert_fusion), kind=kOutput, calls=%fused_computation.5 | convolution fusion | flops 1077936128 | bytes 33555456 | tf_op jit(solution)/shard_map/tij,tjf->tif/dot_general | solution.py:24
  75.8 17.4 %copy.17 = f32[256,128,128]{2,1,0:T(8,128)} copy(f32[256,128,128]{1,2,0:T(8,128)} %multiply_bitcast_fusion.1) | data formatting | bytes 33554432 | tf_op jit(solution)/shard_map/mul | solution.py:25
  93.2 0.2 broadcast_in_dim.10
  93.5 0.0 copy-start.3
  93.5 33.2 %scatter_fusion = f32[32,128,128]{2,1,0:T(8,128)S(1)} fusion(f32[32,128,128]{2,1,0:T(8,128)S(1)} %broadcast_in_dim.10, s32[256]{0:T(256)S(1)} %bitcast.43, f32[256,128,128]{2,1,0:T(8,128)} %copy.17), kind=kCustom, calls=%fused_computation.2 | custom fusion | flops 4194304 | bytes 50332672 | tf_op jit(solution)/shard_map/scatter-add | solution.py:27
  126.7 1.1 convert_element_type.38
  127.8 0.0 reduce-scatter.6.cloned.1.call-update
  127.8 0.0 reduce-scatter.10.cloned.1.call-start
  127.9 74.5 %reduce-scatter.6.cloned.1.call-done = bf16[512,128]{1,0:T(8,128)(2,1)} async-done(((bf16[4096,128]{1,0:T(8,128)(2,1)}), bf16[512,128]{1,0:T(8,128)(2,1)}) %reduce-scatter.6.cloned.1.call-update) | async-done | bytes 131088 | tf_op jit(solution)/shard_map/reduce_scatter | solution.py:29
  202.3 0.0 copy-done
  202.4 1.1 convolution_convert_fusion
  203.5 0.8 copy.22
  204.3 0.0 reduce-scatter.10.cloned.1.call-update
  204.3 0.0 all-gather.6.cloned.1.call-start
  204.4 16.0 %reduce-scatter.10.cloned.1.call-done = bf16[128,512]{1,0:T(8,128)(2,1)} async-done(((bf16[256,512]{1,0:T(8,128)(2,1)}), bf16[128,512]{1,0:T(8,128)(2,1)}) %reduce-scatter.10.cloned.1.call-update) | async-done | bytes 131088
  220.4 1.0 copy.23
  221.4 0.0 copy-done.3
  221.5 0.8 fusion.7
  222.3 5.9 all_gather.16
  228.2 0.9 convolution_convert_fusion.1
  229.0 0.0 all-gather.6.cloned.1.call-update
  229.1 0.0 all-gather.8.cloned.1.call-start
  229.1 1.1 fusion.2
  230.3 0.0 copy-start.2
  230.3 0.7 copy-done.2
  231.0 0.0 all-gather.8.cloned.1.call-update
  231.0 0.2 reduce-scatter.8.cloned.1.call-start
  231.3 50.6 %all-gather.6.cloned.1.call-done = bf16[4096,128]{1,0:T(8,128)(2,1)} async-done(((bf16[512,128]{1,0:T(8,128)(2,1)}), bf16[4096,128]{1,0:T(8,128)(2,1)}) %all-gather.6.cloned.1.call-update) | async-done | bytes 1048592 | tf_op jit(solution)/shard_map/all_gather | solution.py:58
  281.9 9.8 gather_fusion.1
  291.7 15.6 %multiply_bitcast_fusion = f32[256,128,128]{1,2,0:T(8,128)} fusion(bf16[256,128,128]{2,1,0:T(8,128)(2,1)} %gather_fusion.1, bf16[1,1,256,128,128]{4,3,2,1,0:T(8,128)(2,1)} %param.11, f32[256]{0:T(256)S(1)} %compare_convert_fusion), kind=kOutput, calls=%fused_computation.4 | convolution fusion | flops 1077936128 | bytes 33555456 | tf_op jit(solution)/shard_map/tji,tjf->tif/dot_general | solution.py:60
  307.3 17.5 %copy.19 = f32[256,128,128]{2,1,0:T(8,128)} copy(f32[256,128,128]{1,2,0:T(8,128)} %multiply_bitcast_fusion) | data formatting | bytes 33554432 | tf_op jit(solution)/shard_map/mul | solution.py:63
  324.8 2.5 broadcast_in_dim.11
  327.3 52.3 %scatter_fusion.1 = f32[64,128,128]{2,1,0:T(8,128)} fusion(f32[64,128,128]{2,1,0:T(8,128)} %broadcast_in_dim.11, s32[256]{0:T(256)S(1)} %bitcast.42, f32[256,128,128]{2,1,0:T(8,128)} %copy.19), kind=kCustom, calls=%fused_computation.3 | custom fusion | flops 4194304 | bytes 50332672 | tf_op jit(solution)/shard_map/scatter-add | solution.py:65
  379.6 3.9 convert_element_type.46
  383.5 0.0 reduce-scatter.8.cloned.1.call-update
  383.5 695.0 %all-gather.8.cloned.1.call-done = f32[256,2,128,256]{3,2,1,0:T(8,128)} async-done(((f32[1,2,128,256]{3,2,1,0:T(8,128)}), f32[256,2,128,256]{3,2,1,0:T(8,128)}) %all-gather.8.cloned.1.call-update) | async-done | bytes 67108880 | tf_op jit(solution)/shard_map/all_gather | solution.py:51
  1078.5 0.0 copy-start.1
  1078.5 21.2 %reduce_sum.9 = f32[2,128,256]{2,1,0:T(8,128)S(1)} reduce(f32[256,2,128,256]{3,2,1,0:T(8,128)} %all-gather.8.cloned.1.call-done, f32[]{:T(128)} %constant.10.clone.1), dimensions={0}, to_apply=%region_5.6 | reduce | flops 16711680 | bytes 67371008 | tf_op jit(solution)/shard_map/reduce_sum | solution.py:51
  1099.7 0.7 multiply_bitcast_fusion.2
  1100.4 43.4 %reduce-scatter.8.cloned.1.call-done = bf16[512,128]{1,0:T(8,128)(2,1)} async-done(((bf16[8192,128]{1,0:T(8,128)(2,1)}), bf16[512,128]{1,0:T(8,128)(2,1)}) %reduce-scatter.8.cloned.1.call-update) | async-done | bytes 131088 | tf_op jit(solution)/shard_map/reduce_scatter | solution.py:67
  1143.8 0.0 copy-done.1
  (4 shorter events, 0.0 us)
Async XLA Ops:
  7.2 195.2 %copy-start = (bf16[256,256]{1,0:T(8,128)(2,1)S(1)}, bf16[256,256]{1,0:T(8,128)(2,1)}, u32[]{:S(2)}) copy-start(bf16[256,256]{1,0:T(8,128)(2,1)} %param.12) | copy-start | bytes 393220
  7.2 45.4 %all-gather.4.cloned.1.call-start = ((), (), s32[]{:S(2)}) async-start(), calls=%async_computation.3 | async-start | bytes 2228224 | tf_op jit(solution)/shard_map/all_gather | solution.py:22
  7.9 194.4 %reduce-scatter.6.cloned.1.call-start = ((), (), s32[]{:S(2)}) async-start(), calls=%async_computation.4 | async-start | bytes 1179648 | tf_op jit(solution)/shard_map/reduce_scatter | solution.py:29
  93.5 128.0 %copy-start.3 = (bf16[512,128]{1,0:T(8,128)(2,1)S(1)}, bf16[512,128]{1,0:T(8,128)(2,1)}, u32[]{:S(2)}) copy-start(bf16[512,128]{1,0:T(8,128)(2,1)} %param.13) | copy-start | bytes 393220
  127.8 92.6 %reduce-scatter.10.cloned.1.call-start = ((), (), s32[]{:S(2)}) async-start(), calls=%async_computation.8 | async-start | bytes 393216
  204.3 77.5 %all-gather.6.cloned.1.call-start = ((), (), s32[]{:S(2)}) async-start(), calls=%async_computation.5 | async-start | bytes 1179648 | tf_op jit(solution)/shard_map/all_gather | solution.py:58
  229.1 849.5 %all-gather.8.cloned.1.call-start = ((), (), s32[]{:S(2)}) async-start(), calls=%async_computation.7 | async-start | bytes 67371008 | tf_op jit(solution)/shard_map/all_gather | solution.py:51
  230.3 0.7 copy-start.2
  231.0 912.8 %reduce-scatter.8.cloned.1.call-start = ((), (), s32[]{:S(2)}) async-start(), calls=%async_computation.6 | async-start | bytes 2228224 | tf_op jit(solution)/shard_map/reduce_scatter | solution.py:67
  1078.5 65.3 %copy-start.1 = (bf16[256,256]{1,0:T(8,128)(2,1)S(1)}, bf16[256,256]{1,0:T(8,128)(2,1)}, u32[]{:S(2)}) copy-start(bf16[256,256]{1,0:T(8,128)(2,1)} %param.12) | copy-start | bytes 393220
Sparse Core Ops, SparseCore 0:
  9.8 42.6 all-gather.3
  127.9 74.3 reduce-scatter.5
  205.0 15.3 reduce-scatter.9
  229.2 52.6 all-gather.5
  283.6 794.8 all-gather.7
  1081.5 62.2 reduce-scatter.7
